TPU v7x, 32 devices: a whole 2x2x4 slice. The times are simulated.
32 devices in a mesh: level: 4 (over y, x), blk: 8 (over z, core).
Axes of the slice: x: 2, y: 2, z: 4, core: 2. Of those that a mesh axis runs over, the one named last changes fastest.
Arguments:
- right_sides: float32 [4, 512, 2048], P('level', None, 'blk'), may hold values from -6 to 6
- leaf_gen: float32 [4, 2048, 256], P('level', 'blk'), may hold values from -1 to 1, as said below
- leaf_inverse: float32 [4, 1024, 128], P('level', 'blk'), may hold values from -0.5 to 0.5
- leaf_lower: float32 [4, 1024, 128], P('level', 'blk'), may hold values from -0.5 to 0.5
- node_gen: float32 [4, 8, 3, 256, 256], P('level', 'blk'), may hold values from -1 to 1, as said below
- node_inverse: float32 [4, 8, 3, 128, 128], P('level', 'blk'), may hold values from -1 to 1, as said below
- node_lower: float32 [4, 8, 3, 128, 128], P('level', 'blk'), may hold values from -1 to 1, as said below
- coupling: float32 [4, 128, 256], P('level'), may hold values from -0.5 to 0.5
- child_leaf: int32 [4], P('level'), may hold values from 0 to 7
Outputs:
- leaf_solution: float32 [4, 512, 1024], P('level', None, 'blk')
- node_solution: float32 [4, 8, 3, 512, 128], P('level', 'blk')
- root_skeleton: float32 [4, 512, 128], P('level')
Inputs may be any that keep to these rules, and one draw needn't show every extreme that they name: `leaf_gen`: each leaf's 256 x 256 block is orthogonal. node_gen[p, i, h] is orthogonal and equal for all leaves i with the same i >> (h + 1). node_inverse[p, i, h] is equal for all leaves i with the same i >> (h + 1). node_lower[p, i, h] is equal for all leaves i with the same i >> (h + 1).
All inputs are finite; a program needn't handle non-finite values.
Results may differ from a plain program's by a relative error of at most 0.0003.
Values sent between devices are 32-bit elements; how exact they have to be, the bound alone decides.
No kernel may reach another device: no remote copies, remote signals or barrier semaphores. Data moves between devices by JAX's collectives and lax.ppermute only.
A program may use at most 64 MiB of HBM per device.

v0:
```python
import jax
import jax.numpy as jnp
from jax import lax
from jax.sharding import PartitionSpec as P

exact_mode = lax.Precision.HIGHEST


def partner_2(value, axis, distance):
    mask = 2**distance
    pairs = [(source, source ^ mask) for source in range(lax.axis_size(axis))]
    return lax.ppermute(value, axis, pairs)


def broadcast(value, axis, source):
    kept = jnp.where(lax.axis_index(axis) == source, value, 0).astype(value.dtype)
    return lax.psum(kept, axis)


def product(left, right):
    return jnp.matmul(left, right, precision=exact_mode)


def solve_front(
    columns, position, leaf_gen, leaf_inverse, leaf_lower, node_gen, node_inverse, node_lower
):
    redundant = leaf_inverse.shape[2]
    skeleton_size = leaf_lower.shape[2]
    height = node_gen.shape[2]
    turned = product(columns, leaf_gen[0])
    solved = product(turned[:, :redundant], leaf_inverse[0])
    skeleton = turned[:, redundant:] - product(solved, leaf_lower[0])
    node_parts = []
    for tier_index in range(height):
        payload = skeleton
        both = partner_2(payload, "blk", tier_index)
        is_upper = position >> tier_index & 1 == 1
        joined = jnp.where(
            is_upper,
            jnp.concatenate([both, skeleton], axis=1),
            jnp.concatenate([skeleton, both], axis=1),
        )
        generator = node_gen[0, 0, tier_index]
        turned_node = product(joined, generator)
        node_solved = product(turned_node[:, :skeleton_size], node_inverse[0, 0, tier_index])
        skeleton = turned_node[:, skeleton_size:] - product(
            node_solved, node_lower[0, 0, tier_index]
        )
        node_parts.append(node_solved)
    return (solved, jnp.stack(node_parts), skeleton)


def compose_maps(
    position, coupling, leaf_gen, leaf_inverse, leaf_lower, node_gen, node_inverse, node_lower
):
    redundant = leaf_inverse.shape[2]
    skeleton_size = leaf_lower.shape[2]
    height = node_gen.shape[2]
    lifted = product(coupling[0], leaf_gen[0])
    leaf_map = product(lifted[:, :redundant], leaf_inverse[0])
    carried = lifted[:, redundant:] - product(leaf_map, leaf_lower[0])
    tier_maps = []
    for tier_index in range(height):
        is_upper = position >> tier_index & 1 == 1
        generator = node_gen[0, 0, tier_index]
        half_rows = jnp.where(is_upper, generator[skeleton_size:], generator[:skeleton_size])
        turned = product(carried, half_rows)
        node_map = product(turned[:, :skeleton_size], node_inverse[0, 0, tier_index])
        carried = turned[:, skeleton_size:] - product(node_map, node_lower[0, 0, tier_index])
        tier_maps.append(node_map)
    return (leaf_map, jnp.stack(tier_maps), carried)


def shards(
    right_sides,
    leaf_gen,
    leaf_inverse,
    leaf_lower,
    node_gen,
    node_inverse,
    node_lower,
    coupling,
    child_leaf,
):
    column_total = right_sides.shape[1]
    skeleton_size = leaf_lower.shape[2]
    height = node_gen.shape[2]
    level_index = lax.axis_index("level")
    position = lax.axis_index("blk")
    is_target = position == child_leaf[0]
    tiers = jnp.arange(height, dtype=jnp.int32)
    in_subtree = (position >> tiers + 1 == child_leaf[0] >> tiers + 1)[:, None, None]
    solved, stacked, skeleton = solve_front(
        right_sides[0],
        position,
        leaf_gen,
        leaf_inverse,
        leaf_lower,
        node_gen,
        node_inverse,
        node_lower,
    )
    leaf_map, tier_maps, root_map = compose_maps(
        position, coupling, leaf_gen, leaf_inverse, leaf_lower, node_gen, node_inverse, node_lower
    )
    tier_maps, root_map = (
        broadcast(tier_maps, "blk", child_leaf[0]),
        broadcast(root_map, "blk", child_leaf[0]),
    )
    all_maps, all_roots = (
        lax.all_gather(root_map[None], "level", axis=0, tiled=True),
        lax.all_gather(skeleton[None], "level", axis=0, tiled=True),
    )

    def advance(earlier, paired):
        latest = paired[1] + product(earlier, paired[0])
        return (latest, earlier)

    final_root, incomings = lax.scan(
        advance, jnp.zeros((column_total, skeleton_size), jnp.float32), (all_maps, all_roots)
    )
    incoming = lax.dynamic_index_in_dim(incomings, level_index, 0, keepdims=False)
    leaf_part = solved + jnp.where(is_target, product(incoming, leaf_map), 0.0)
    node_part = stacked + jnp.where(in_subtree, product(incoming[None], tier_maps), 0.0)
    root_part = skeleton + product(incoming, root_map)
    return (leaf_part[None], node_part[None, None], root_part[None])


def solution(mesh):
    in_specs = (
        P("level", None, "blk"),
        P("level", "blk", None),
        P("level", "blk", None),
        P("level", "blk", None),
        P("level", "blk", None, None, None),
        P("level", "blk", None, None, None),
        P("level", "blk", None, None, None),
        P("level", None, None),
        P("level"),
    )
    out_specs = (
        P("level", None, "blk"),
        P("level", "blk", None, None, None),
        P("level", None, None),
    )
    return jax.shard_map(shards, mesh=mesh, in_specs=in_specs, out_specs=out_specs, check_vma=False)
```

profile of v0, /device:TPU:0, one launch (start us, length us, event | category | flops | bytes accessed | tf_op | source)
XLA Modules:
  0.0 122.1 jit_solution(14816391280824697077)
XLA Ops:
  8.1 1.0 copy-done
  9.0 1.6 %fusion.33 = f32[512,256]{0,1:T(8,128)S(1)} fusion(f32[1,512,256]{2,1,0:T(8,128)S(1)} %copy-done, f32[1,256,256]{2,1,0:T(8,128)} %param.12), kind=kOutput, calls=%fused_computation.47 | convolution fusion | flops 402653184 | bytes 1310720 | tf_op jit(solution)/shard_map/dot_general | solution.py:21
  10.7 0.6 fusion.41
  11.3 0.2 copy-done.8
  11.5 0.4 convolution_subtract_fusion
  11.9 0.6 collective-permute-start
  12.5 0.3 fusion.49
  12.8 0.2 fusion.83
  13.0 0.2 convolution_subtract_fusion.4
  13.2 0.3 fusion.65
  13.5 0.6 copy-done.4
  14.4 0.2 convolution_subtract_fusion.3
  14.6 0.3 fusion.63
  14.9 0.2 fusion.79
  15.3 0.7 fusion.15
  16.0 0.6 fusion.39
  16.6 0.4 slice_subtract_fusion.2
  17.0 2.7 %collective-permute-start.1 = (f32[512,128]{0,1:T(8,128)S(1)}, f32[512,128]{0,1:T(8,128)S(1)}, u32[]{:S(2)}, u32[]{:S(2)}) collective-permute-start(f32[512,128]{0,1:T(8,128)S(1)} %slice_subtract_fusion.2), channel_id=1, source_target_pairs={{0,2},{1,3},{2,0},{3,1},{4,6},{5,7},{6,4},{7,5},{8,10},{9,11},{10,... | collective-permute-start | bytes 786440 | tf_op jit(solution)/shard_map/ppermute | solution.py:12
  19.7 0.3 fusion.61
  20.8 5.8 %collective-permute-done.1 = f32[512,128]{0,1:T(8,128)S(1)} collective-permute-done((f32[512,128]{0,1:T(8,128)S(1)}, f32[512,128]{0,1:T(8,128)S(1)}, u32[]{:S(2)}, u32[]{:S(2)}) %collective-permute-start.1) | collective-permute-done | bytes 262176 | tf_op jit(solution)/shard_map/ppermute | solution.py:12
  26.6 0.7 fusion.21
  27.3 0.6 fusion.37
  27.9 0.4 slice_subtract_fusion.1
  28.3 2.8 %collective-permute-start.2 = (f32[512,128]{0,1:T(8,128)S(1)}, f32[512,128]{0,1:T(8,128)S(1)}, u32[]{:S(2)}, u32[]{:S(2)}) collective-permute-start(f32[512,128]{0,1:T(8,128)S(1)} %slice_subtract_fusion.1), channel_id=1, source_target_pairs={{0,4},{1,5},{2,6},{3,7},{4,0},{5,1},{6,2},{7,3},{8,12},{9,13},{10,... | collective-permute-start | bytes 786440 | tf_op jit(solution)/shard_map/ppermute | solution.py:12
  31.1 0.7 maximum_select_fusion.6
  31.8 0.8 fusion.14
  32.7 10.8 %collective-permute-done.2 = f32[512,128]{0,1:T(8,128)S(1)} collective-permute-done((f32[512,128]{0,1:T(8,128)S(1)}, f32[512,128]{0,1:T(8,128)S(1)}, u32[]{:S(2)}, u32[]{:S(2)}) %collective-permute-start.2) | collective-permute-done | bytes 262176 | tf_op jit(solution)/shard_map/ppermute | solution.py:12
  43.5 1.0 fusion.27
  44.5 0.4 fusion.35
  44.9 1.1 slice_subtract_fusion
  46.0 42.8 %all-reduce.3.cloned.1.call-done = (f32[128,128]{1,0:T(8,128)}, f32[3,128,128]{2,1,0:T(8,128)}) async-done(((f32[128,128]{1,0:T(8,128)}, f32[3,128,128]{2,1,0:T(8,128)}), (f32[128,128]{1,0:T(8,128)}, f32[3,128,128]{2,1,0:T(8,128)})) %all-reduce.3.cloned.1.call-update) | async-done | bytes 262160 | tf_op jit(solution)/shard_map/psum | solution.py:17
  88.8 9.3 %all-gather.1 = f32[512,128]{1,0:T(8,128)S(1)} all-gather(f32[128,128]{1,0:T(8,128)} %get-tuple-element.64), channel_id=3, replica_groups=mesh['level'=4,'blk'=8] {'level'}, dimensions={0}, use_global_device_ids=true | all-gather | bytes 327680 | tf_op jit(solution)/shard_map/all_gather | solution.py:111
  98.1 9.3 %while.13 = (s32[]{:T(128)}, f32[512,128]{0,1:T(8,128)S(1)}, f32[4,512,128]{1,2,0:T(8,128)}, f32[4,512,128]{2,1,0:T(8,128)}, f32[4,128,128]{2,1,0:T(8,128)S(1)}, /*index=5*/s32[]{:T(128)}, s32[]{:T(128)}) while((s32[]{:T(128)}, f32[512,128]{0,1:T(8,128)S(1)}, f32[4,512,128]{1,2,0:T(8,128)}, f32[4,512,128]{2,1,0:T(8,128)}, ...), condition=%wide.region_2.3_spmd.clone, body=%wide.region_1.2_spmd.clone.sunk | while | flops 100859904 | bytes 2949228 | solution.py:119
  98.1 1.0 constant_dynamic-slice_fusion.2
  99.2 0.7 bitcast_dynamic-update-slice_fusion.2
  100.0 0.4 fusion.150
  100.4 1.0 constant_dynamic-slice_fusion.2
  101.6 0.7 bitcast_dynamic-update-slice_fusion.2
  102.3 0.4 fusion.150
  102.8 1.0 constant_dynamic-slice_fusion.2
  103.9 0.7 bitcast_dynamic-update-slice_fusion.2
  104.6 0.4 fusion.150
  105.1 1.0 constant_dynamic-slice_fusion.2
  106.2 0.7 bitcast_dynamic-update-slice_fusion.2
  106.9 0.4 fusion.150
  107.4 2.3 %fusion.13 = f32[1,512,128]{2,1,0:T(8,128)} fusion(f32[512,128]{1,0:T(8,128)S(1)} %fusion.41, f32[128,128]{1,0:T(8,128)S(1)} %fusion.83, f32[4,512,128]{1,2,0:T(8,128)} %get-tuple-element.30, s32[]{:T(128)S(6)} %select_n.102, pred[]{:T(512)S(6)} %eq.24), kind=kOutput, calls=%fused_computation.19 | convolution fusion | flops 100794368 | bytes 851973 | tf_op jit(solution)/shard_map/dot_general | solution.py:21
  109.7 2.3 %fusion.11 = f32[1,512,128]{2,1,0:T(8,128)} fusion(f32[512,128]{1,0:T(8,128)S(1)} %copy-done.1, f32[128,128]{1,0:T(8,128)S(1)} %copy-done.7, f32[4,512,128]{1,2,0:T(8,128)} %get-tuple-element.30, s32[]{:T(128)S(6)} %select_n.102), kind=kOutput, calls=%fused_computation.16 | convolution fusion | flops 100728832 | bytes 851972 | tf_op jit(solution)/shard_map/dot_general | solution.py:21
  112.0 2.7 %fusion.10 = f32[1,1,3,512,128]{4,3,2,1,0:T(8,128)} fusion(f32[3,128,128]{2,1,0:T(8,128)S(1)} %copy-done.9, f32[1,512,128]{2,1,0:T(8,128)S(1)} %bitcast.144, f32[1,512,128]{2,1,0:T(8,128)S(1)} %bitcast.143, f32[1,512,128]{2,1,0:T(8,128)S(1)} %bitcast.142, pred[3]{0:T(512)(128)(4,1)S(1)} %shift-right-arithmetic_compare_fusion, ...), kind=kOutput, calls=%fused_computation.14 | convolution fusion | flops 302776320 | bytes 2031623 | tf_op jit(solution)/shard_map/dot_general | solution.py:21
  (39 shorter events, 1.4 us)
Async XLA Ops:
  8.0 1.0 copy-start
  8.0 2.6 %copy-start.6 = (f32[1,128,128]{2,1,0:T(8,128)S(1)}, f32[1,128,128]{2,1,0:T(8,128)}, u32[]{:S(2)}) copy-start(f32[1,128,128]{2,1,0:T(8,128)} %param.13) | copy-start | bytes 196612
  8.0 80.8 %all-reduce.3.cloned.1.call-start = ((), (), s32[]{:S(2)}) async-start(), calls=%async_computation.1 | async-start | bytes 524288 | tf_op jit(solution)/shard_map/psum | solution.py:17
  10.7 0.8 copy-start.8
  10.7 1.8 %copy-start.3 = (f32[1,256,256]{2,1,0:T(8,128)S(1)}, f32[1,256,256]{2,1,0:T(8,128)}, u32[]{:S(2)}) copy-start(f32[1,256,256]{2,1,0:T(8,128)} %param.12) | copy-start | bytes 786436
  10.7 1.8 %copy-start.10 = (f32[1,128,256]{2,1,0:T(8,128)S(1)}, f32[1,128,256]{2,1,0:T(8,128)}, u32[]{:S(2)}) copy-start(f32[1,128,256]{2,1,0:T(8,128)} %param.18) | copy-start | bytes 393220
  11.5 1.7 %copy-start.2 = (f32[1,1,3,256,256]{4,3,2,1,0:T(8,128)S(1)}, f32[1,1,3,256,256]{4,3,2,1,0:T(8,128)}, u32[]{:S(2)}) copy-start(f32[1,1,3,256,256]{4,3,2,1,0:T(8,128)} %param.15) | copy-start | bytes 2359300
  11.9 3.4 %collective-permute-start = (f32[512,128]{0,1:T(8,128)S(1)}, f32[512,128]{0,1:T(8,128)S(1)}, u32[]{:S(2)}, u32[]{:S(2)}) collective-permute-start(f32[512,128]{0,1:T(8,128)S(1)} %convolution_subtract_fusion), channel_id=1, source_target_pairs={{0,1},{1,0},{2,3},{3,2},{4,5},{5,4},{6,7},{7,6},{8,9},{9,8},{10,11... | collective-permute-start | bytes 786440 | tf_op jit(solution)/shard_map/ppermute | solution.py:12
  13.2 0.9 copy-start.4
  13.2 1.1 copy-start.5
  17.0 9.6 %collective-permute-start.1 = (f32[512,128]{0,1:T(8,128)S(1)}, f32[512,128]{0,1:T(8,128)S(1)}, u32[]{:S(2)}, u32[]{:S(2)}) collective-permute-start(f32[512,128]{0,1:T(8,128)S(1)} %slice_subtract_fusion.2), channel_id=1, source_target_pairs={{0,2},{1,3},{2,0},{3,1},{4,6},{5,7},{6,4},{7,5},{8,10},{9,11},{10,... | collective-permute-start | bytes 786440 | tf_op jit(solution)/shard_map/ppermute | solution.py:12
  28.3 15.2 %collective-permute-start.2 = (f32[512,128]{0,1:T(8,128)S(1)}, f32[512,128]{0,1:T(8,128)S(1)}, u32[]{:S(2)}, u32[]{:S(2)}) collective-permute-start(f32[512,128]{0,1:T(8,128)S(1)} %slice_subtract_fusion.1), channel_id=1, source_target_pairs={{0,4},{1,5},{2,6},{3,7},{4,0},{5,1},{6,2},{7,3},{8,12},{9,13},{10,... | collective-permute-start | bytes 786440 | tf_op jit(solution)/shard_map/ppermute | solution.py:12
  32.7 65.4 %all-gather.4.cloned.1.call-start = ((), (), s32[]{:S(2)}) async-start(), calls=%async_computation | async-start | bytes 1310720 | tf_op jit(solution)/shard_map/all_gather | solution.py:112
  107.4 2.3 %copy-start.1 = (f32[512,128]{1,0:T(8,128)S(1)}, f32[512,128]{1,0:T(8,128)}, u32[]{:S(2)}) copy-start(f32[512,128]{1,0:T(8,128)} %slice_subtract_fusion) | copy-start | bytes 786436
  107.4 2.3 %copy-start.7 = (f32[128,128]{1,0:T(8,128)S(1)}, f32[128,128]{1,0:T(8,128)}, u32[]{:S(2)}) copy-start(f32[128,128]{1,0:T(8,128)} %get-tuple-element.64) | copy-start | bytes 196612
  109.7 2.3 %copy-start.9 = (f32[3,128,128]{2,1,0:T(8,128)S(1)}, f32[3,128,128]{2,1,0:T(8,128)}, u32[]{:S(2)}) copy-start(f32[3,128,128]{2,1,0:T(8,128)} %get-tuple-element.65) | copy-start | bytes 589828
Sparse Core Ops, SparseCore 0:
  32.8 55.9 all-reduce.2
Sparse Core Ops, SparseCore 1:
  46.1 27.6 all-gather.3
where the time goes:
time: 123 us; the launch traced here: 122 us
  waiting for transfers between devices  59.4 us (48%)
  matrix products  20.7 us (17%)
  between operations  16.5 us (13%)
  blocking collectives  9.25 us (8%)
  local copies, waits for them, and re-layouts  6.36 us (5%)
  starting transfers between devices  6.12 us (5%)
  other arithmetic  3.64 us (3%)
    psum x1, waiting for transfers between devices, broadcast(): return lax.psum(kept, axis)  42.8 us
    dot_general x31, matrix products, product(): return jnp.matmul(left, right, precision=exact_mode)  20.7 us
    ppermute x3, waiting for transfers between devices, partner_2(): return lax.ppermute(value, axis, pairs)  16.6 us
    all_gather x1, blocking collectives, shards(): lax.all_gather(root_map[None], 'level', axis=0, tiled=True)  9.25 us
    ppermute x3, starting transfers between devices, partner_2(): return lax.ppermute(value, axis, pairs)  6.03 us
    dynamic_slice x8, local copies, waits for them, and re-layouts, shards(): lax.scan(advance, jnp.zeros((column_total, skeleton_size), jnp.float32),...  4.41 us
    dynamic_update_slice x4, other arithmetic, shards(): lax.scan(advance, jnp.zeros((column_total, skeleton_size), jnp.float32),...  2.93 us
  transfers between devices with their start and end apart: 5, of which 3 were waited for; matrix products, arithmetic and copies ran while one was open for 5% of the time, Pallas kernels for 0%

commit v1 on v0

--- a/solution.py
+++ b/solution.py
@@ -14,7 +14,7 @@
 
 def broadcast(value, axis, source):
     kept = jnp.where(lax.axis_index(axis) == source, value, 0).astype(value.dtype)
-    return lax.psum(kept, axis)
+    return jnp.sum(lax.all_gather(kept, axis), axis=0)
 
 
 def product(left, right):

time: 123 us -> 112 us (0.911)
  waiting for transfers between devices: 59.4 us -> 32.2 us
  blocking collectives: 9.25 us -> 26.2 us
  other arithmetic: 3.64 us -> 5.17 us
  between operations: 16.5 us -> 15 us
    psum x1 -> x0, waiting for transfers between devices: 42.8 us -> none  [broadcast(): return lax.psum(kept, axis)]
    all_gather x0 -> x1, blocking collectives: none -> 14.8 us  [broadcast(): return jnp.sum(lax.all_gather(kept, axis), axis=0)]
    all_gather x0 -> x1, waiting for transfers between devices: none -> 13.6 us  [broadcast(): return jnp.sum(lax.all_gather(kept, axis), axis=0)]
    all_gather x1, blocking collectives: 9.25 us -> 11.4 us  [shards(): lax.all_gather(root_map[None], 'level', axis=0, tiled=True)]
    ppermute x3, waiting for transfers between devices: 16.6 us -> 18.3 us  [partner_2(): return lax.ppermute(value, axis, pairs)]
    reduce_sum x0 -> x2, other arithmetic: none -> 1.53 us  [broadcast(): return jnp.sum(lax.all_gather(kept, axis), axis=0)]
  transfers between devices with their start and end apart: 5 -> 5, of which waited for: 3 -> 5; matrix products, arithmetic and copies ran while one was open for 5% -> 15% of each run, Pallas kernels for 0% -> 0%
where the time goes in v1:
time: 112 us
  waiting for transfers between devices  32.2 us (29%)
  blocking collectives  26.2 us (23%)
  matrix products  20.9 us (19%)
  between operations  15 us (13%)
  starting transfers between devices  6.46 us (6%)
  local copies, waits for them, and re-layouts  5.54 us (5%)
  other arithmetic  5.17 us (5%)
    dot_general x31, matrix products, product(): return jnp.matmul(left, right, precision=exact_mode)  20.9 us
    ppermute x3, waiting for transfers between devices, partner_2(): return lax.ppermute(value, axis, pairs)  18.3 us
    all_gather x1, blocking collectives, broadcast(): return jnp.sum(lax.all_gather(kept, axis), axis=0)  14.8 us
    all_gather x1, waiting for transfers between devices, broadcast(): return jnp.sum(lax.all_gather(kept, axis), axis=0)  13.6 us
    all_gather x1, blocking collectives, shards(): lax.all_gather(root_map[None], 'level', axis=0, tiled=True)  11.4 us
    ppermute x3, starting transfers between devices, partner_2(): return lax.ppermute(value, axis, pairs)  6.38 us
    dynamic_slice x8, local copies, waits for them, and re-layouts, shards(): lax.scan(advance, jnp.zeros((column_total, skeleton_size), jnp.float32),...  4.45 us
    dynamic_update_slice x4, other arithmetic, shards(): lax.scan(advance, jnp.zeros((column_total, skeleton_size), jnp.float32),...  2.93 us
  transfers between devices with their start and end apart: 5, of which 5 were waited for; matrix products, arithmetic and copies ran while one was open for 15% of the time, Pallas kernels for 0%

profile of v1, /device:TPU:0, one launch (start us, length us, event | category | flops | bytes accessed | tf_op | source)
XLA Modules:
  0.0 111.6 jit_solution(5999122725552073250)
XLA Ops:
  7.2 1.0 copy-done
  8.2 1.6 %fusion.33 = f32[512,256]{0,1:T(8,128)S(1)} fusion(f32[1,512,256]{2,1,0:T(8,128)S(1)} %copy-done, f32[1,256,256]{2,1,0:T(8,128)} %param.12), kind=kOutput, calls=%fused_computation.47 | convolution fusion | flops 402653184 | bytes 1310720 | tf_op jit(solution)/shard_map/dot_general | solution.py:21
  9.8 1.5 %fusion.41 = f32[512,128]{1,0:T(8,128)S(1)} fusion(f32[512,256]{0,1:T(8,128)S(1)} %fusion.33, f32[1,128,128]{2,1,0:T(8,128)} %param.13), kind=kOutput, calls=%fused_computation.58 | convolution fusion | flops 100663296 | bytes 589824 | tf_op jit(solution)/shard_map/dot_general | solution.py:21
  11.3 0.4 convolution_subtract_fusion
  11.8 0.6 collective-permute-start
  12.3 1.2 %collective-permute-done = f32[512,128]{0,1:T(8,128)S(1)} collective-permute-done((f32[512,128]{0,1:T(8,128)S(1)}, f32[512,128]{0,1:T(8,128)S(1)}, u32[]{:S(2)}, u32[]{:S(2)}) %collective-permute-start) | collective-permute-done | bytes 262176 | tf_op jit(solution)/shard_map/ppermute | solution.py:12
  13.5 0.7 fusion.15
  14.2 0.6 fusion.39
  14.8 0.4 slice_subtract_fusion.2
  15.2 3.0 %collective-permute-start.1 = (f32[512,128]{0,1:T(8,128)S(1)}, f32[512,128]{0,1:T(8,128)S(1)}, u32[]{:S(2)}, u32[]{:S(2)}) collective-permute-start(f32[512,128]{0,1:T(8,128)S(1)} %slice_subtract_fusion.2), channel_id=1, source_target_pairs={{0,2},{1,3},{2,0},{3,1},{4,6},{5,7},{6,4},{7,5},{8,10},{9,11},{10,... | collective-permute-start | bytes 786440 | tf_op jit(solution)/shard_map/ppermute | solution.py:12
  18.2 0.3 fusion.49
  18.8 6.1 %collective-permute-done.1 = f32[512,128]{0,1:T(8,128)S(1)} collective-permute-done((f32[512,128]{0,1:T(8,128)S(1)}, f32[512,128]{0,1:T(8,128)S(1)}, u32[]{:S(2)}, u32[]{:S(2)}) %collective-permute-start.1) | collective-permute-done | bytes 262176 | tf_op jit(solution)/shard_map/ppermute | solution.py:12
  24.8 0.7 fusion.21
  25.5 0.6 fusion.37
  26.1 0.4 slice_subtract_fusion.1
  26.5 2.8 %collective-permute-start.2 = (f32[512,128]{0,1:T(8,128)S(1)}, f32[512,128]{0,1:T(8,128)S(1)}, u32[]{:S(2)}, u32[]{:S(2)}) collective-permute-start(f32[512,128]{0,1:T(8,128)S(1)} %slice_subtract_fusion.1), channel_id=1, source_target_pairs={{0,4},{1,5},{2,6},{3,7},{4,0},{5,1},{6,2},{7,3},{8,12},{9,13},{10,... | collective-permute-start | bytes 786440 | tf_op jit(solution)/shard_map/ppermute | solution.py:12
  29.6 0.3 fusion.65
  29.9 11.0 %collective-permute-done.2 = f32[512,128]{0,1:T(8,128)S(1)} collective-permute-done((f32[512,128]{0,1:T(8,128)S(1)}, f32[512,128]{0,1:T(8,128)S(1)}, u32[]{:S(2)}, u32[]{:S(2)}) %collective-permute-start.2) | collective-permute-done | bytes 262176 | tf_op jit(solution)/shard_map/ppermute | solution.py:12
  40.9 1.0 fusion.27
  41.9 0.4 fusion.35
  42.3 1.1 slice_subtract_fusion
  44.5 0.3 fusion.63
  44.7 0.2 fusion.79
  45.0 0.2 convolution_subtract_fusion.2
  45.2 0.3 fusion.61
  45.4 0.2 fusion.77
  45.7 0.7 maximum_select_fusion.6
  46.6 14.8 %all-gather.1 = f32[1024,128]{1,0:T(8,128)S(1)} all-gather(f32[128,128]{1,0:T(8,128)S(1)} %fusion.14), channel_id=3, replica_groups=mesh['level'=4,'blk'=8] {'blk'}, dimensions={0}, use_global_device_ids=true | all-gather | bytes 589824 | tf_op jit(solution)/shard_map/all_gather | solution.py:17
  61.4 11.4 %all-gather.2 = f32[512,128]{1,0:T(8,128)S(1)} all-gather(f32[128,128]{1,0:T(8,128)S(1)} %reduce_sum.18), channel_id=4, replica_groups=mesh['level'=4,'blk'=8] {'level'}, dimensions={0}, use_global_device_ids=true | all-gather | bytes 327680 | tf_op jit(solution)/shard_map/all_gather | solution.py:111
  72.9 0.3 all-gather.8.cloned.1.call-done
  73.1 9.3 %while.13 = (s32[]{:T(128)}, f32[512,128]{0,1:T(8,128)S(1)}, f32[4,512,128]{1,2,0:T(8,128)}, f32[4,512,128]{2,1,0:T(8,128)}, f32[4,128,128]{2,1,0:T(8,128)S(1)}, /*index=5*/s32[]{:T(128)}, s32[]{:T(128)}) while((s32[]{:T(128)}, f32[512,128]{0,1:T(8,128)S(1)}, f32[4,512,128]{1,2,0:T(8,128)}, f32[4,512,128]{2,1,0:T(8,128)}, ...), condition=%wide.region_2.3_spmd.clone, body=%wide.region_1.2_spmd.clone.sunk | while | flops 100859904 | bytes 2949228 | solution.py:119
  73.2 1.0 constant_dynamic-slice_fusion.2
  74.3 0.7 bitcast_dynamic-update-slice_fusion.2
  75.0 0.4 fusion.150
  75.5 1.0 constant_dynamic-slice_fusion.2
  76.6 0.7 bitcast_dynamic-update-slice_fusion.2
  77.4 0.4 fusion.150
  77.8 1.0 constant_dynamic-slice_fusion.2
  79.0 0.7 bitcast_dynamic-update-slice_fusion.2
  79.7 0.4 fusion.150
  80.2 1.0 constant_dynamic-slice_fusion.2
  81.3 0.7 bitcast_dynamic-update-slice_fusion.2
  82.0 0.4 fusion.150
  82.5 2.2 %fusion.11 = f32[1,512,128]{2,1,0:T(8,128)} fusion(f32[512,128]{1,0:T(8,128)S(1)} %copy-done.1, f32[128,128]{1,0:T(8,128)S(1)} %reduce_sum.18, f32[4,512,128]{1,2,0:T(8,128)} %get-tuple-element.30, s32[]{:T(128)S(6)} %select_n.109), kind=kOutput, calls=%fused_computation.16 | convolution fusion | flops 100728832 | bytes 851972 | tf_op jit(solution)/shard_map/dot_general | solution.py:21
  84.7 2.2 %fusion.13 = f32[1,512,128]{2,1,0:T(8,128)} fusion(f32[512,128]{1,0:T(8,128)S(1)} %fusion.41, f32[128,128]{1,0:T(8,128)S(1)} %fusion.83, f32[4,512,128]{1,2,0:T(8,128)} %get-tuple-element.30, s32[]{:T(128)S(6)} %select_n.109, pred[]{:T(512)S(6)} %eq.24), kind=kOutput, calls=%fused_computation.19 | convolution fusion | flops 100794368 | bytes 851973 | tf_op jit(solution)/shard_map/dot_general | solution.py:21
  87.0 13.6 %all-gather.6.cloned.1.call-done = f32[8,3,128,128]{3,2,1,0:T(8,128)} async-done(((f32[1,3,128,128]{3,2,1,0:T(8,128)}), f32[8,3,128,128]{3,2,1,0:T(8,128)}) %all-gather.6.cloned.1.call-update) | async-done | bytes 1572880 | tf_op jit(solution)/shard_map/all_gather | solution.py:17
  100.6 1.5 %reduce_sum.19 = f32[3,128,128]{2,1,0:T(8,128)S(1)} reduce(f32[8,3,128,128]{3,2,1,0:T(8,128)} %all-gather.6.cloned.1.call-done, f32[]{:T(128)} %constant.18.clone.1), dimensions={0}, to_apply=%region_3.4 | reduce | flops 344064 | bytes 1769476 | tf_op jit(solution)/shard_map/reduce_sum | solution.py:17
  102.1 2.7 %fusion.10 = f32[1,1,3,512,128]{4,3,2,1,0:T(8,128)} fusion(f32[3,128,128]{2,1,0:T(8,128)S(1)} %reduce_sum.19, f32[1,512,128]{2,1,0:T(8,128)S(1)} %bitcast.145, f32[1,512,128]{2,1,0:T(8,128)S(1)} %bitcast.144, f32[1,512,128]{2,1,0:T(8,128)S(1)} %bitcast.143, pred[3]{0:T(512)(128)(4,1)S(1)} %shift-right-arithmetic_compare_fusion, ...), kind=kOutput, calls=%fused_computation.14 | convolution fusion | flops 302776320 | bytes 2031623 | tf_op jit(solution)/shard_map/dot_general | solution.py:21
  (38 shorter events, 1.8 us)
Async XLA Ops:
  7.2 1.0 copy-start
  7.2 4.2 %copy-start.7 = (f32[1,128,128]{2,1,0:T(8,128)S(1)}, f32[1,128,128]{2,1,0:T(8,128)}, u32[]{:S(2)}) copy-start(f32[1,128,128]{2,1,0:T(8,128)} %param.14) | copy-start | bytes 196612
  7.2 6.3 %copy-start.2 = (f32[1,1,3,256,256]{4,3,2,1,0:T(8,128)S(1)}, f32[1,1,3,256,256]{4,3,2,1,0:T(8,128)}, u32[]{:S(2)}) copy-start(f32[1,1,3,256,256]{4,3,2,1,0:T(8,128)} %param.15) | copy-start | bytes 2359300
  7.2 65.9 %all-gather.8.cloned.1.call-start = ((), (), s32[]{:S(2)}) async-start(), calls=%async_computation.1 | async-start | bytes 1310720 | tf_op jit(solution)/shard_map/all_gather | solution.py:112
  9.8 4.4 %copy-start.4 = (f32[1,1,3,128,128]{4,3,2,1,0:T(8,128)S(1)}, f32[1,1,3,128,128]{4,3,2,1,0:T(8,128)}, u32[]{:S(2)}) copy-start(f32[1,1,3,128,128]{4,3,2,1,0:T(8,128)} %param.16) | copy-start | bytes 589828
  9.8 5.0 %copy-start.5 = (f32[1,1,3,128,128]{4,3,2,1,0:T(8,128)S(1)}, f32[1,1,3,128,128]{4,3,2,1,0:T(8,128)}, u32[]{:S(2)}) copy-start(f32[1,1,3,128,128]{4,3,2,1,0:T(8,128)} %param.17) | copy-start | bytes 589828
  11.8 6.5 %copy-start.3 = (f32[1,256,256]{2,1,0:T(8,128)S(1)}, f32[1,256,256]{2,1,0:T(8,128)}, u32[]{:S(2)}) copy-start(f32[1,256,256]{2,1,0:T(8,128)} %param.12) | copy-start | bytes 786436
  11.8 6.5 %copy-start.8 = (f32[1,128,256]{2,1,0:T(8,128)S(1)}, f32[1,128,256]{2,1,0:T(8,128)}, u32[]{:S(2)}) copy-start(f32[1,128,256]{2,1,0:T(8,128)} %param.18) | copy-start | bytes 393220
  11.8 1.7 %collective-permute-start = (f32[512,128]{0,1:T(8,128)S(1)}, f32[512,128]{0,1:T(8,128)S(1)}, u32[]{:S(2)}, u32[]{:S(2)}) collective-permute-start(f32[512,128]{0,1:T(8,128)S(1)} %convolution_subtract_fusion), channel_id=1, source_target_pairs={{0,1},{1,0},{2,3},{3,2},{4,5},{5,4},{6,7},{7,6},{8,9},{9,8},{10,11... | collective-permute-start | bytes 786440 | tf_op jit(solution)/shard_map/ppermute | solution.py:12
  12.3 6.2 %copy-start.6 = (f32[1,128,128]{2,1,0:T(8,128)S(1)}, f32[1,128,128]{2,1,0:T(8,128)}, u32[]{:S(2)}) copy-start(f32[1,128,128]{2,1,0:T(8,128)} %param.13) | copy-start | bytes 196612
  15.2 9.6 %collective-permute-start.1 = (f32[512,128]{0,1:T(8,128)S(1)}, f32[512,128]{0,1:T(8,128)S(1)}, u32[]{:S(2)}, u32[]{:S(2)}) collective-permute-start(f32[512,128]{0,1:T(8,128)S(1)} %slice_subtract_fusion.2), channel_id=1, source_target_pairs={{0,2},{1,3},{2,0},{3,1},{4,6},{5,7},{6,4},{7,5},{8,10},{9,11},{10,... | collective-permute-start | bytes 786440 | tf_op jit(solution)/shard_map/ppermute | solution.py:12
  26.5 14.3 %collective-permute-start.2 = (f32[512,128]{0,1:T(8,128)S(1)}, f32[512,128]{0,1:T(8,128)S(1)}, u32[]{:S(2)}, u32[]{:S(2)}) collective-permute-start(f32[512,128]{0,1:T(8,128)S(1)} %slice_subtract_fusion.1), channel_id=1, source_target_pairs={{0,4},{1,5},{2,6},{3,7},{4,0},{5,1},{6,2},{7,3},{8,12},{9,13},{10,... | collective-permute-start | bytes 786440 | tf_op jit(solution)/shard_map/ppermute | solution.py:12
  43.3 57.2 %all-gather.6.cloned.1.call-start = ((), (), s32[]{:S(2)}) async-start(), calls=%async_computation | async-start | bytes 1769472 | tf_op jit(solution)/shard_map/all_gather | solution.py:17
  73.1 9.3 %copy-start.1 = (f32[512,128]{1,0:T(8,128)S(1)}, f32[512,128]{1,0:T(8,128)}, u32[]{:S(2)}) copy-start(f32[512,128]{1,0:T(8,128)} %slice_subtract_fusion) | copy-start | bytes 786436
Sparse Core Ops, SparseCore 0:
  43.5 29.6 all-gather.7
  75.3 25.1 all-gather.5
